TPU v7x, 32 devices: a whole 2x2x4 slice. The times are simulated.
32 devices in a mesh: grp: 4 (over x, core), ep: 4 (over z), sq: 2 (over y).
Axes of the slice: x: 2, y: 2, z: 4, core: 2. Of those that a mesh axis runs over, the one named last changes fastest.
Arguments:
- queries: bfloat16 [8192, 2048], P(('grp', 'ep', 'sq')), may hold values from -32 to 32
- keys: bfloat16 [8192, 512], P(('grp', 'ep', 'sq')), may hold values from -32 to 32
- values: bfloat16 [8192, 512], P(('grp', 'ep', 'sq')), may hold values from -6 to 6
- norm_gain: float32 [2048], replicated, may hold values from 0.1 to 1.9
- expert_ids: int32 [8192, 2], P(('grp', 'ep', 'sq')), may hold values from 0 to 3, all different within a row; in each aligned block of 256 rows (0 to 255, 256 to 511, ...) at most 192 rows name the same one
- gate_values: float32 [8192, 2], P(('grp', 'ep', 'sq')), may hold values from 0.1 to 1
- hidden_grad: bfloat16 [8192, 1024], P(('grp', 'ep', 'sq')), may hold values from -0.59765625 to 0.59765625
- gate_weight: bfloat16 [4, 2048, 1024], P('ep', None, 'sq'), may hold values from -0.125 to 0.125
- up_weight: bfloat16 [4, 2048, 1024], P('ep', None, 'sq'), may hold values from -0.125 to 0.125
Outputs:
- gate_grad: float32 [4, 2048, 1024], P('ep', 'grp', 'sq')
Inputs may be any that keep to these rules, and one draw needn't show every extreme that they name: `expert_ids`: each token names 2 different experts; within the 256 tokens of one device no expert is named more than 192 times.
All inputs are finite; a program needn't handle non-finite values.
Results may differ from a plain program's by a relative error of at most 0.0085.
Values may be sent and summed in bfloat16 or wider, within the bound.
A program may use at most 64 MiB of HBM per device.

v0:
```python
import math
import jax
import jax.numpy as jnp
from jax import lax
from jax.sharding import PartitionSpec as P

HEAD_DIM = 128
LENGTH = 512
epsilon = 1e-05
masked_score = -1e30


def gate_term(inputs, cotangent, weight_gate, weight_up):
    pre_gate = jnp.dot(inputs, weight_gate, preferred_element_type=jnp.float32)
    pre_up = jnp.dot(inputs, weight_up, preferred_element_type=jnp.float32)
    sigmoid_gate = jax.nn.sigmoid(pre_gate)
    slope = sigmoid_gate * (1.0 + pre_gate * (1.0 - sigmoid_gate))
    delta_gate = (cotangent.astype(jnp.float32) * pre_up * slope).astype(jnp.bfloat16)
    return lax.dot_general(
        inputs, delta_gate, (((0,), (0,)), ((), ())), preferred_element_type=jnp.float32
    )


def body(
    queries, keys, values, norm_gain, expert_ids, gate_values, hidden_grad, gate_weight, up_weight
):
    rows_here, model_width = queries.shape
    kv_width = keys.shape[1]
    kv_heads = kv_width // HEAD_DIM
    group_size = model_width // kv_width
    score_scale = 1.0 / math.sqrt(HEAD_DIM)
    shard_index = lax.axis_index("sq")
    query_positions = shard_index * rows_here + jnp.arange(rows_here, dtype=jnp.int32)
    query_sequence = query_positions // LENGTH
    query_heads = queries.reshape(rows_here, kv_heads, group_size, HEAD_DIM)
    running_max = jnp.full((rows_here, kv_heads, group_size), masked_score, jnp.float32)
    key_rows = lax.all_gather(keys, "sq", axis=0, tiled=True)
    value_rows = lax.all_gather(values, "sq", axis=0, tiled=True)
    key_count = key_rows.shape[0]
    key_heads = key_rows.reshape(key_count, kv_heads, HEAD_DIM)
    value_heads = value_rows.reshape(key_count, kv_heads, HEAD_DIM)
    scores = (
        jnp.einsum("tkgd,rkd->tkgr", query_heads, key_heads, preferred_element_type=jnp.float32)
        * score_scale
    )
    key_positions = jnp.arange(key_count, dtype=jnp.int32)
    causal = key_positions[None, :] <= query_positions[:, None]
    same_sequence = (key_positions // LENGTH)[None, :] == query_sequence[:, None]
    allowed = (causal & same_sequence)[:, None, None, :]
    scores = jnp.where(allowed, scores, masked_score)
    updated_max = jnp.maximum(running_max, jnp.max(scores, axis=-1))
    exponent_terms = jnp.where(allowed, jnp.exp(scores - updated_max[..., None]), 0.0)
    running_sum = jnp.sum(exponent_terms, axis=-1)
    running_out = jnp.einsum(
        "tkgr,rkd->tkgd",
        exponent_terms.astype(jnp.bfloat16),
        value_heads,
        preferred_element_type=jnp.float32,
    )
    attended = (running_out / running_sum[..., None]).reshape(rows_here, model_width)
    mean_square = jnp.mean(attended * attended, axis=-1, keepdims=True)
    normed = (attended * lax.rsqrt(mean_square + epsilon) * norm_gain).astype(jnp.bfloat16)
    top_count = expert_ids.shape[1]
    experts = lax.axis_size("ep")
    capacity = rows_here * top_count // experts * 3 // 2
    hidden_width = hidden_grad.shape[1]
    flat_ids = expert_ids.reshape(-1)
    one_hot = (flat_ids[:, None] == jnp.arange(experts, dtype=jnp.int32)[None, :]).astype(jnp.int32)
    slot_rank = jnp.sum(jnp.cumsum(one_hot, axis=0) * one_hot, axis=1) - 1
    slot_target = flat_ids * capacity + slot_rank
    routed_inputs = jnp.repeat(normed, top_count, axis=0)
    routed_grad = (
        gate_values.reshape(-1, 1) * jnp.repeat(hidden_grad, top_count, axis=0).astype(jnp.float32)
    ).astype(jnp.bfloat16)
    send_inputs = (
        jnp.zeros((experts * capacity, model_width), jnp.bfloat16)
        .at[slot_target]
        .set(routed_inputs)
    )
    send_grad = (
        jnp.zeros((experts * capacity, hidden_width), jnp.bfloat16).at[slot_target].set(routed_grad)
    )
    send_inputs = send_inputs.reshape(experts, capacity, model_width)
    send_grad = send_grad.reshape(experts, capacity, hidden_width)
    got_inputs, got_grad = (
        lax.all_to_all(send_inputs, "ep", split_axis=0, concat_axis=0, tiled=True),
        lax.all_to_all(send_grad, "ep", split_axis=0, concat_axis=0, tiled=True),
    )
    expert_inputs = got_inputs.reshape(-1, model_width)
    expert_grad = got_grad.reshape(-1, hidden_width)
    weight_gate = gate_weight[0]
    weight_up = up_weight[0]
    local_hidden = weight_gate.shape[1]
    column_start = shard_index * local_hidden
    input_rows = lax.all_gather(expert_inputs, "sq", axis=0, tiled=True)
    grad_rows = lax.all_gather(expert_grad, "sq", axis=0, tiled=True)
    cotangent = lax.dynamic_slice_in_dim(grad_rows, column_start, local_hidden, 1)
    summed = gate_term(input_rows, cotangent, weight_gate, weight_up)
    return lax.psum_scatter(
        summed[None].astype(jnp.bfloat16), "grp", scatter_dimension=1, tiled=True
    ).astype(jnp.float32)


def solution(mesh):
    return jax.shard_map(
        body,
        mesh=mesh,
        in_specs=(
            P(("grp", "ep", "sq"), None),
            P(("grp", "ep", "sq"), None),
            P(("grp", "ep", "sq"), None),
            P(),
            P(("grp", "ep", "sq"), None),
            P(("grp", "ep", "sq"), None),
            P(("grp", "ep", "sq"), None),
            P("ep", None, "sq"),
            P("ep", None, "sq"),
        ),
        out_specs=P("ep", "grp", "sq"),
        check_vma=False,
    )
```

profile of v0, /device:TPU:0, one launch (start us, length us, event | category | flops | bytes accessed | tf_op | source)
XLA Modules:
  0.0 312.1 jit_solution(6690040816627483020)
XLA Ops:
  6.5 0.8 broadcast_multiply_fusion
  7.4 0.8 copy.15
  8.6 0.1 mul.78
  8.8 1.2 reduce-window.6
  10.0 0.2 slice_reduce_fusion
  10.2 0.2 reduce-window.9
  10.5 1.1 copy.17
  11.6 10.0 %all_gather.12 = bf16[512,512]{0,1:T(8,128)(2,1)} all-gather(bf16[256,512]{0,1:T(8,128)(2,1)S(1)} %copy.17), channel_id=1, replica_groups=mesh['grp'=4,'ep'=4,'sq'=2] {'sq'}, dimensions={0}, use_global_device_ids=true | all-gather | bytes 786432 | tf_op jit(solution)/shard_map/all_gather | solution.py:37
  21.7 8.4 %all_gather.13 = bf16[512,512]{1,0:T(8,128)(2,1)S(1)} all-gather(bf16[256,512]{1,0:T(8,128)(2,1)} %param.11), channel_id=1, replica_groups=mesh['grp'=4,'ep'=4,'sq'=2] {'sq'}, dimensions={0}, use_global_device_ids=true | all-gather | bytes 786432 | tf_op jit(solution)/shard_map/all_gather | solution.py:38
  30.0 1.0 copy.20
  31.0 1.8 reshape.173
  32.8 0.2 fusion.25
  33.0 2.7 fusion
  35.8 2.0 fusion.1
  37.8 2.5 multiply_reduce_fusion
  40.3 1.3 fusion.13
  41.7 1.5 copy.22
  43.1 2.6 broadcast_in_dim.51
  45.8 4.1 %reshape.185 = bf16[512,2048]{1,0:T(8,128)(2,1)} reshape(bf16[256,2,2048]{2,1,0:T(2,128)(2,1)} %broadcast_in_dim.51) | data formatting | bytes 4194304 | tf_op jit(solution)/shard_map/reshape | solution.py:71
  49.9 6.7 %scatter_custom_fusion = bf16[768,2048]{1,0:T(8,128)(2,1)} fusion(s32[512]{0:T(512)S(1)} %bitcast.79, bf16[512,2048]{1,0:T(8,128)(2,1)} %reshape.185, bf16[]{:T(256)} %constant.25.clone.1), kind=kCustom, calls=%fused_computation.23 | custom fusion | bytes 3146240 | tf_op jit(solution)/shard_map/scatter | solution.py:78
  56.6 74.8 %all_to_all.10 = bf16[4,192,2048]{2,1,0:T(8,128)(2,1)} all-to-all(bf16[4,192,2048]{2,1,0:T(8,128)(2,1)} %bitcast.72), channel_id=1, replica_groups=mesh['grp'=4,'ep'=4,'sq'=2] {'ep'}, dimensions={0} | all-to-all | bytes 6291456 | tf_op jit(solution)/shard_map/all_to_all | solution.py:86
  131.5 0.6 copy-done.4
  132.5 2.0 broadcast_in_dim.53
  134.4 3.7 %convert_element_type.40 = f32[512,1024]{1,0:T(8,128)} reshape(f32[256,2,1024]{2,1,0:T(2,128)} %broadcast_in_dim.53) | data formatting | bytes 4194304 | tf_op jit(solution)/shard_map/convert_element_type | solution.py:73
  138.1 5.3 %scatter_custom_fusion.1 = bf16[768,1024]{1,0:T(8,128)(2,1)} fusion(s32[512]{0:T(512)S(1)} %bitcast.80, f32[512,1024]{1,0:T(8,128)} %convert_element_type.40, f32[512]{0:T(512)S(1)} %mul.89, bf16[]{:T(256)} %constant.25.clone.1), kind=kCustom, calls=%fused_computation.25 | custom fusion | flops 1048576 | bytes 3672066 | tf_op jit(solution)/shard_map/scatter | solution.py:81
  143.4 40.3 %all_to_all.11 = bf16[4,192,1024]{2,1,0:T(8,128)(2,1)} all-to-all(bf16[4,192,1024]{2,1,0:T(8,128)(2,1)} %bitcast.74), channel_id=1, replica_groups=mesh['grp'=4,'ep'=4,'sq'=2] {'ep'}, dimensions={0} | all-to-all | bytes 3145728 | tf_op jit(solution)/shard_map/all_to_all | solution.py:87
  183.7 26.9 %all-gather.3.cloned.1.call-done = bf16[1536,2048]{1,0:T(8,128)(2,1)} async-done(((bf16[768,2048]{1,0:T(8,128)(2,1)}), bf16[1536,2048]{1,0:T(8,128)(2,1)}) %all-gather.3.cloned.1.call-update) | async-done | bytes 6291472 | tf_op jit(solution)/shard_map/all_gather | solution.py:95
  210.7 8.5 %fusion.9 = f32[1536,512]{1,0:T(8,128)} fusion(bf16[1536,2048]{1,0:T(8,128)(2,1)} %all-gather.3.cloned.1.call-done, bf16[1,2048,512]{2,1,0:T(8,128)(2,1)} %param.16), kind=kOutput, calls=%fused_computation.14 | convolution fusion | flops 3221225472 | bytes 11534336 | tf_op jit(solution)/shard_map/dot_general | solution.py:14
  219.2 38.0 %all-gather.5.cloned.1.call-done = bf16[1536,1024]{1,0:T(8,128)(2,1)} async-done(((bf16[768,1024]{1,0:T(8,128)(2,1)}), bf16[1536,1024]{1,0:T(8,128)(2,1)}) %all-gather.5.cloned.1.call-update) | async-done | bytes 3145744 | tf_op jit(solution)/shard_map/all_gather | solution.py:96
  257.2 14.6 %fusion.8 = bf16[1,2048,512]{2,1,0:T(8,128)(2,1)} fusion(bf16[1536,2048]{1,0:T(8,128)(2,1)} %all-gather.3.cloned.1.call-done, f32[1536,512]{1,0:T(8,128)} %fusion.9, bf16[1,2048,512]{2,1,0:T(8,128)(2,1)S(1)} %copy-done, bf16[1536,1024]{1,0:T(8,128)(2,1)} %all-gather.5.cloned.1.call-done, s32[]{:T(128)S(6)} %select_n.44), kind=kOutput, calls=%fused_computation.13 | convolution fusion | flops 6452150272 | bytes 21495812 | tf_op jit(solution)/shard_map/dot_general | solution.py:19
  271.8 31.6 %reduce-scatter.2.cloned.1.call-done = bf16[1,512,512]{2,1,0:T(8,128)(2,1)} async-done(((bf16[1,2048,512]{2,1,0:T(8,128)(2,1)}), bf16[1,512,512]{2,1,0:T(8,128)(2,1)}) %reduce-scatter.2.cloned.1.call-update) | async-done | bytes 524304 | tf_op jit(solution)/shard_map/reduce_scatter | solution.py:99
  303.4 2.1 convert_element_type.46
  (29 shorter events, 1.1 us)
Async XLA Ops:
  6.5 250.7 %copy-start = (bf16[1,2048,512]{2,1,0:T(8,128)(2,1)S(1)}, bf16[1,2048,512]{2,1,0:T(8,128)(2,1)}, u32[]{:S(2)}) copy-start(bf16[1,2048,512]{2,1,0:T(8,128)(2,1)} %param.17) | copy-start | bytes 6291460
  6.5 204.1 %all-gather.3.cloned.1.call-start = ((), (), s32[]{:S(2)}) async-start(), calls=%async_computation.3 | async-start | bytes 9437184 | tf_op jit(solution)/shard_map/all_gather | solution.py:95
  35.8 2.0 copy-start.2
  37.8 2.5 copy-start.3
  131.4 0.7 copy-start.4
  131.4 1.1 copy-start.1
  131.4 125.8 %all-gather.5.cloned.1.call-start = ((), (), s32[]{:S(2)}) async-start(), calls=%async_computation.4 | async-start | bytes 4718592 | tf_op jit(solution)/shard_map/all_gather | solution.py:96
  183.7 119.7 %reduce-scatter.2.cloned.1.call-start = ((), (), s32[]{:S(2)}) async-start(), calls=%async_computation.5 | async-start | bytes 2621440 | tf_op jit(solution)/shard_map/reduce_scatter | solution.py:99
Sparse Core Ops, SparseCore 0:
  131.6 79.0 all-gather.2
  212.2 44.9 all-gather.4
  272.0 31.4 reduce-scatter.1
where the time goes:
time: 313 us; the launch traced here: 312 us
  blocking collectives  133 us (42%)
  waiting for transfers between devices  96.5 us (31%)
  matrix products  28.4 us (9%)
  local copies, waits for them, and re-layouts  27 us (9%)
  other arithmetic  13.3 us (4%)
  between operations  13.3 us (4%)
    all_to_all x1, blocking collectives, body(): lax.all_to_all(send_inputs, 'ep', split_axis=0, concat_axis=0, tiled=True)  74.8 us
    all_to_all x1, blocking collectives, body(): lax.all_to_all(send_grad, 'ep', split_axis=0, concat_axis=0, tiled=True)  40.3 us
    all_gather x1, waiting for transfers between devices, body(): grad_rows = lax.all_gather(expert_grad, 'sq', axis=0, tiled=True)  38 us
    reduce_scatter x1, waiting for transfers between devices, body(): lax.psum_scatter(summed[None].astype(jnp.bfloat16), 'grp', scatter_dimens...  31.6 us
    all_gather x1, waiting for transfers between devices, body(): input_rows = lax.all_gather(expert_inputs, 'sq', axis=0, tiled=True)  26.9 us
    dot_general x1, matrix products, gate_term(): lax.dot_general(inputs, delta_gate, (((0,), (0,)), ((), ())), preferred_e...  14.6 us
    all_gather x1, blocking collectives, body(): key_rows = lax.all_gather(keys, 'sq', axis=0, tiled=True)  10 us
    dot_general x1, matrix products, gate_term(): pre_gate = jnp.dot(inputs, weight_gate, preferred_element_type=jnp.float32)  8.55 us
  transfers between devices with their start and end apart: 3, of which 3 were waited for; matrix products, arithmetic and copies ran while one was open for 6% of the time, Pallas kernels for 0%

commit v1 on v0

--- a/solution.py
+++ b/solution.py
@@ -8,6 +8,22 @@
 LENGTH = 512
 epsilon = 1e-05
 masked_score = -1e30
+
+
+def pairwise_exchange(shard, axis, split, join):
+    ways, here = (lax.axis_size(axis), lax.axis_index(axis))
+    width = shard.shape[split] // ways
+    lengths = list(shard.shape)
+    lengths[split] = width
+    height = lengths[join]
+    lengths[join] = height * ways
+    full = jnp.zeros(lengths, shard.dtype)
+    for mask in range(ways):
+        part = lax.dynamic_slice_in_dim(shard, (here ^ mask) * width, width, axis=split)
+        if mask:
+            part = lax.ppermute(part, axis, [(d, d ^ mask) for d in range(ways)])
+        full = lax.dynamic_update_slice_in_dim(full, part, (here ^ mask) * height, axis=join)
+    return full
 
 
 def gate_term(inputs, cotangent, weight_gate, weight_up):
@@ -83,7 +99,7 @@
     send_inputs = send_inputs.reshape(experts, capacity, model_width)
     send_grad = send_grad.reshape(experts, capacity, hidden_width)
     got_inputs, got_grad = (
-        lax.all_to_all(send_inputs, "ep", split_axis=0, concat_axis=0, tiled=True),
+        pairwise_exchange(send_inputs, "ep", 0, 0),
         lax.all_to_all(send_grad, "ep", split_axis=0, concat_axis=0, tiled=True),
     )
     expert_inputs = got_inputs.reshape(-1, model_width)

time: 313 us -> 319 us (1.019)
  blocking collectives: 133 us -> 68.5 us
  waiting for transfers between devices: 96.5 us -> 152 us
  local copies, waits for them, and re-layouts: 27 us -> 34.1 us
  starting transfers between devices: 0.09 us -> 4.47 us
    all_to_all x1 -> x0, blocking collectives: 74.8 us -> none  [body(): lax.all_to_all(send_inputs, 'ep', split_axis=0, concat_axis=0, tiled=True)]
    ppermute x0 -> x3, waiting for transfers between devices: none -> 51.2 us  [pairwise_exchange(): part = lax.ppermute(part, axis, [(d, d ^ mask) for d in range(ways)])]
    all_to_all x1, blocking collectives: 40.3 us -> 50.4 us  [body(): lax.all_to_all(send_grad, 'ep', split_axis=0, concat_axis=0, tiled=True)]
    ppermute x0 -> x3, starting transfers between devices: none -> 4.39 us  [pairwise_exchange(): part = lax.ppermute(part, axis, [(d, d ^ mask) for d in range(ways)])]
    all_gather x1, waiting for transfers between devices: 26.9 us -> 31.1 us  [body(): input_rows = lax.all_gather(expert_inputs, 'sq', axis=0, tiled=True)]
  transfers between devices with their start and end apart: 3 -> 6, of which waited for: 3 -> 5; matrix products, arithmetic and copies ran while one was open for 6% -> 7% of each run, Pallas kernels for 0% -> 0%
where the time goes in v1:
time: 319 us; the launch traced here: 318 us
  waiting for transfers between devices  152 us (48%)
  blocking collectives  68.5 us (21%)
  local copies, waits for them, and re-layouts  34.1 us (11%)
  matrix products  30.5 us (10%)
  other arithmetic  15.4 us (5%)
  between operations  13.3 us (4%)
  starting transfers between devices  4.47 us (1%)
    ppermute x3, waiting for transfers between devices, pairwise_exchange(): part = lax.ppermute(part, axis, [(d, d ^ mask) for d in range(ways)])  51.2 us
    all_to_all x1, blocking collectives, body(): lax.all_to_all(send_grad, 'ep', split_axis=0, concat_axis=0, tiled=True)  50.4 us
    all_gather x1, waiting for transfers between devices, body(): grad_rows = lax.all_gather(expert_grad, 'sq', axis=0, tiled=True)  38 us
    reduce_scatter x1, waiting for transfers between devices, body(): lax.psum_scatter(summed[None].astype(jnp.bfloat16), 'grp', scatter_dimens...  31.6 us
    all_gather x1, waiting for transfers between devices, body(): input_rows = lax.all_gather(expert_inputs, 'sq', axis=0, tiled=True)  31.1 us
    dot_general x1, matrix products, gate_term(): lax.dot_general(inputs, delta_gate, (((0,), (0,)), ((), ())), preferred_e...  14.6 us
    all_gather x1, blocking collectives, body(): key_rows = lax.all_gather(keys, 'sq', axis=0, tiled=True)  9.94 us
    dot_general x1, matrix products, gate_term(): pre_gate = jnp.dot(inputs, weight_gate, preferred_element_type=jnp.float32)  8.48 us
  transfers between devices with their start and end apart: 6, of which 5 were waited for; matrix products, arithmetic and copies ran while one was open for 7% of the time, Pallas kernels for 0%

profile of v1, /device:TPU:0, one launch (start us, length us, event | category | flops | bytes accessed | tf_op | source)
XLA Modules:
  0.0 318.2 jit_solution(6170619024243081111)
XLA Ops:
  8.5 1.8 reshape.173
  10.3 1.1 copy.17
  11.4 9.9 %all_gather.12 = bf16[512,512]{0,1:T(8,128)(2,1)S(1)} all-gather(bf16[256,512]{0,1:T(8,128)(2,1)S(1)} %copy.17), channel_id=1, replica_groups=mesh['grp'=4,'ep'=4,'sq'=2] {'sq'}, dimensions={0}, use_global_device_ids=true | all-gather | bytes 786432 | tf_op jit(solution)/shard_map/all_gather | solution.py:53
  21.5 4.9 %fusion = (f32[256,4,4]{0,2,1:T(4,128)S(1)}, f32[4,512,256,4]{2,1,3,0:T(8,128)}) fusion(pred[256,512]{0,1:T(8,128)(4,1)S(1)} %fusion.25, bf16[512,4,128,1]{0,2,3,1:T(8,128)(2,1)S(1)} %bitcast.72, bf16[256,4,4,128]{3,2,1,0:T(4,128)(2,1)S(1)} %reshape.173), kind=kOutput, calls=%fused_computation.4 | convolution fusion | flops 543158272 | bytes 10108928 | tf_op jit(solution)/shard_map/tkgd,rkd->tkgr/dot_general | solution.py:59
  26.4 8.2 %all_gather.13 = bf16[512,512]{1,0:T(8,128)(2,1)S(1)} all-gather(bf16[256,512]{1,0:T(8,128)(2,1)S(1)} %copy-done.4), channel_id=1, replica_groups=mesh['grp'=4,'ep'=4,'sq'=2] {'sq'}, dimensions={0}, use_global_device_ids=true | all-gather | bytes 786432 | tf_op jit(solution)/shard_map/all_gather | solution.py:54
  34.8 4.6 %fusion.1 = f32[256,4,4]{0,2,1:T(4,128)S(1)} fusion(f32[4,512,256,4]{2,1,3,0:T(8,128)} %get-tuple-element.10, f32[256,4,4]{0,2,1:T(4,128)S(1)} %broadcast_maximum_fusion, pred[256,512]{0,1:T(8,128)(4,1)S(1)} %fusion.25), kind=kLoop, calls=%fused_computation.5 | loop fusion | flops 10481664 | bytes 8552448 | tf_op jit(solution)/shard_map/reduce_sum | solution.py:69
  39.4 1.2 copy-done.1
  40.7 2.5 multiply_reduce_fusion
  43.2 1.3 fusion.13
  44.5 1.5 copy.22
  46.0 2.6 broadcast_in_dim.55
  48.6 4.1 %reshape.185 = bf16[512,2048]{1,0:T(8,128)(2,1)} reshape(bf16[256,2,2048]{2,1,0:T(2,128)(2,1)} %broadcast_in_dim.55) | data formatting | bytes 4194304 | tf_op jit(solution)/shard_map/reshape | solution.py:87
  52.7 1.2 reduce-window.6
  54.8 6.7 %scatter_custom_fusion = bf16[768,2048]{1,0:T(8,128)(2,1)} fusion(s32[512]{0:T(512)S(1)} %bitcast.76, bf16[512,2048]{1,0:T(8,128)(2,1)} %reshape.185, bf16[]{:T(256)} %constant.25.clone.1), kind=kCustom, calls=%fused_computation.23 | custom fusion | bytes 3146240 | tf_op jit(solution)/shard_map/scatter | solution.py:94
  61.5 2.0 broadcast_in_dim.49
  63.5 1.0 copy-done.2
  64.5 1.3 constant_dynamic-slice_fusion
  65.8 1.5 collective-permute-start
  67.3 2.6 collective-permute-start.1
  70.1 28.6 %collective-permute-done = bf16[1,192,2048]{2,1,0:T(8,128)(2,1)S(1)} collective-permute-done((bf16[1,192,2048]{2,1,0:T(8,128)(2,1)S(1)}, bf16[1,192,2048]{2,1,0:T(8,128)(2,1)S(1)}, u32[]{:S(2)}, u32[]{:S(2)}) %collective-permute-start) | collective-permute-done | bytes 786464 | tf_op jit(solution)/shard_map/ppermute | solution.py:24
  98.7 1.0 constant_dynamic-update-slice_fusion.2
  99.7 22.6 %collective-permute-done.1 = bf16[1,192,2048]{2,1,0:T(8,128)(2,1)S(1)} collective-permute-done((bf16[1,192,2048]{2,1,0:T(8,128)(2,1)S(1)}, bf16[1,192,2048]{2,1,0:T(8,128)(2,1)S(1)}, u32[]{:S(2)}, u32[]{:S(2)}) %collective-permute-start.1) | collective-permute-done | bytes 786464 | tf_op jit(solution)/shard_map/ppermute | solution.py:24
  124.4 1.9 broadcast_in_dim.57
  126.3 3.7 %convert_element_type.40 = f32[512,1024]{1,0:T(8,128)} reshape(f32[256,2,1024]{2,1,0:T(2,128)} %broadcast_in_dim.57) | data formatting | bytes 4194304 | tf_op jit(solution)/shard_map/convert_element_type | solution.py:89
  130.3 4.9 %scatter_custom_fusion.1 = bf16[768,1024]{1,0:T(8,128)(2,1)} fusion(s32[512]{0:T(512)S(1)} %bitcast.77, f32[512,1024]{1,0:T(8,128)} %convert_element_type.40, f32[512]{0:T(512)S(1)} %mul.89, bf16[]{:T(256)} %constant.25.clone.1), kind=kCustom, calls=%fused_computation.25 | custom fusion | flops 1048576 | bytes 3672066 | tf_op jit(solution)/shard_map/scatter | solution.py:97
  135.2 50.4 %all_to_all.5 = bf16[4,192,1024]{2,1,0:T(8,128)(2,1)} all-to-all(bf16[4,192,1024]{2,1,0:T(8,128)(2,1)} %bitcast.71), channel_id=1, replica_groups=mesh['grp'=4,'ep'=4,'sq'=2] {'ep'}, dimensions={0} | all-to-all | bytes 3145728 | tf_op jit(solution)/shard_map/all_to_all | solution.py:103
  185.7 31.1 %all-gather.3.cloned.1.call-done = bf16[1536,2048]{1,0:T(8,128)(2,1)} async-done(((bf16[768,2048]{1,0:T(8,128)(2,1)}), bf16[1536,2048]{1,0:T(8,128)(2,1)}) %all-gather.3.cloned.1.call-update) | async-done | bytes 6291472 | tf_op jit(solution)/shard_map/all_gather | solution.py:111
  216.8 8.5 %fusion.9 = f32[1536,512]{1,0:T(8,128)} fusion(bf16[1536,2048]{1,0:T(8,128)(2,1)} %all-gather.3.cloned.1.call-done, bf16[1,2048,512]{2,1,0:T(8,128)(2,1)} %param.16), kind=kOutput, calls=%fused_computation.14 | convolution fusion | flops 3221225472 | bytes 11534336 | tf_op jit(solution)/shard_map/dot_general | solution.py:30
  225.2 38.0 %all-gather.5.cloned.1.call-done = bf16[1536,1024]{1,0:T(8,128)(2,1)} async-done(((bf16[768,1024]{1,0:T(8,128)(2,1)}), bf16[1536,1024]{1,0:T(8,128)(2,1)}) %all-gather.5.cloned.1.call-update) | async-done | bytes 3145744 | tf_op jit(solution)/shard_map/all_gather | solution.py:112
  263.3 14.6 %fusion.8 = bf16[1,2048,512]{2,1,0:T(8,128)(2,1)} fusion(bf16[1536,2048]{1,0:T(8,128)(2,1)} %all-gather.3.cloned.1.call-done, f32[1536,512]{1,0:T(8,128)} %fusion.9, bf16[1,2048,512]{2,1,0:T(8,128)(2,1)S(1)} %copy-done, bf16[1536,1024]{1,0:T(8,128)(2,1)} %all-gather.5.cloned.1.call-done, s32[]{:T(128)S(6)} %select_n.64), kind=kOutput, calls=%fused_computation.13 | convolution fusion | flops 6452150272 | bytes 21495812 | tf_op jit(solution)/shard_map/dot_general | solution.py:35
  277.9 31.6 %reduce-scatter.2.cloned.1.call-done = bf16[1,512,512]{2,1,0:T(8,128)(2,1)} async-done(((bf16[1,2048,512]{2,1,0:T(8,128)(2,1)}), bf16[1,512,512]{2,1,0:T(8,128)(2,1)}) %reduce-scatter.2.cloned.1.call-update) | async-done | bytes 524304 | tf_op jit(solution)/shard_map/reduce_scatter | solution.py:115
  309.5 2.1 convert_element_type.46
  (43 shorter events, 5.8 us)
Async XLA Ops:
  6.5 256.7 %copy-start = (bf16[1,2048,512]{2,1,0:T(8,128)(2,1)S(1)}, bf16[1,2048,512]{2,1,0:T(8,128)(2,1)}, u32[]{:S(2)}) copy-start(bf16[1,2048,512]{2,1,0:T(8,128)(2,1)} %param.17) | copy-start | bytes 6291460
  6.5 210.2 %all-gather.3.cloned.1.call-start = ((), (), s32[]{:S(2)}) async-start(), calls=%async_computation.2 | async-start | bytes 9437184 | tf_op jit(solution)/shard_map/all_gather | solution.py:111
  21.5 4.9 %copy-start.4 = (bf16[256,512]{1,0:T(8,128)(2,1)S(1)}, bf16[256,512]{1,0:T(8,128)(2,1)}, u32[]{:S(2)}) copy-start(bf16[256,512]{1,0:T(8,128)(2,1)} %param.11) | copy-start | bytes 786436
  34.8 5.8 %copy-start.1 = (f32[4,512,256,4]{2,1,3,0:T(8,128)S(1)}, f32[4,512,256,4]{2,1,3,0:T(8,128)}, u32[]{:S(2)}) copy-start(f32[4,512,256,4]{2,1,3,0:T(8,128)} %get-tuple-element.10) | copy-start | bytes 25165828
  40.7 2.5 copy-start.5
  61.5 3.0 copy-start.2
  65.8 33.0 %collective-permute-start = (bf16[1,192,2048]{2,1,0:T(8,128)(2,1)S(1)}, bf16[1,192,2048]{2,1,0:T(8,128)(2,1)S(1)}, u32[]{:S(2)}, u32[]{:S(2)}) collective-permute-start(bf16[1,192,2048]{2,1,0:T(8,128)(2,1)S(1)} %get-tuple-element.7), channel_id=1, source_target_pairs={{0,2},{2,0},{4,6},{6,4},{1,3},{3,1},{5,7},{7,5},{8,10},{10,8},{12,... | collective-permute-start | bytes 2359304 | tf_op jit(solution)/shard_map/ppermute | solution.py:24
  67.3 55.1 %collective-permute-start.1 = (bf16[1,192,2048]{2,1,0:T(8,128)(2,1)S(1)}, bf16[1,192,2048]{2,1,0:T(8,128)(2,1)S(1)}, u32[]{:S(2)}, u32[]{:S(2)}) collective-permute-start(bf16[1,192,2048]{2,1,0:T(8,128)(2,1)S(1)} %get-tuple-element.6), channel_id=1, source_target_pairs={{0,4},{2,6},{4,0},{6,2},{1,5},{3,7},{5,1},{7,3},{8,12},{10,14},{12... | collective-permute-start | bytes 2359304 | tf_op jit(solution)/shard_map/ppermute | solution.py:24
  69.8 53.5 %collective-permute-start.2 = (bf16[1,192,2048]{2,1,0:T(8,128)(2,1)S(1)}, bf16[1,192,2048]{2,1,0:T(8,128)(2,1)S(1)}, u32[]{:S(2)}, u32[]{:S(2)}) collective-permute-start(bf16[1,192,2048]{2,1,0:T(8,128)(2,1)S(1)} %get-tuple-element.5), channel_id=1, source_target_pairs={{0,6},{2,4},{4,2},{6,0},{1,7},{3,5},{5,3},{7,1},{8,14},{10,12},{12... | collective-permute-start | bytes 2359304 | tf_op jit(solution)/shard_map/ppermute | solution.py:24
  99.7 24.7 %copy-start.3 = (bf16[256,1024]{1,0:T(8,128)(2,1)S(1)}, bf16[256,1024]{1,0:T(8,128)(2,1)}, u32[]{:S(2)}) copy-start(bf16[256,1024]{1,0:T(8,128)(2,1)} %param.15) | copy-start | bytes 1572868
  124.3 5.6 %copy-start.6 = (f32[256,2]{0,1:T(2,128)S(1)}, f32[256,2]{0,1:T(2,128)}, u32[]{:S(2)}) copy-start(f32[256,2]{0,1:T(2,128)} %param.14) | copy-start | bytes 6148
  124.4 138.9 %all-gather.5.cloned.1.call-start = ((), (), s32[]{:S(2)}) async-start(), calls=%async_computation.3 | async-start | bytes 4718592 | tf_op jit(solution)/shard_map/all_gather | solution.py:112
  185.6 123.9 %reduce-scatter.2.cloned.1.call-start = ((), (), s32[]{:S(2)}) async-start(), calls=%async_computation.4 | async-start | bytes 2621440 | tf_op jit(solution)/shard_map/reduce_scatter | solution.py:115
Sparse Core Ops, SparseCore 0:
  124.5 92.2 all-gather.2
  218.3 44.9 all-gather.4
  278.0 31.4 reduce-scatter.1
